TPU v7x, 256 devices: a whole 4x4x8 slice. The times are simulated.
256 devices in a mesh: dp: 4 (over x), mp: 64 (over z, y, core).
Axes of the slice: x: 4, y: 4, z: 8, core: 2. Of those that a mesh axis runs over, the one named last changes fastest.
Arguments:
- residual: bfloat16 [1024, 4096], P(('dp', 'mp')), may hold values from -6 to 6
- ffn_gain: float32 [4096], replicated, may hold values from 0.5 to 1.5
- gate_weight: bfloat16 [4096, 8192], P(None, 'mp'), may hold values from -0.09375 to 0.09375
- up_weight: bfloat16 [4096, 8192], P(None, 'mp'), may hold values from -0.09375 to 0.09375
- down_weight: bfloat16 [8192, 4096], P('mp'), may hold values from -0.0625 to 0.0625
- final_gain: float32 [4096], replicated, may hold values from 0.5 to 1.5
- head_weight: bfloat16 [4096, 65536], P(None, 'mp')
- passage_ids: int32 [4, 256], P('dp'), may hold values from 0 to 3, never falling along the last dimension, each value on 1 to 128 neighbouring positions
- valid_counts: int32 [4, 4], P('dp'), may hold values from 1 to 128
Outputs:
- term_weights: float32 [16, 65536], P('dp', 'mp')
- entropy: float32 [], replicated
- grad_hidden: float32 [1024, 4096], P(('dp', 'mp'))
Inputs may be any that keep to these rules, and one draw needn't show every extreme that they name: `passage_ids`: within each group the ids never fall and every passage of 0 to 3 has 1 to 128 rows.
All inputs are finite; a program needn't handle non-finite values.
Results may differ from a plain program's by a relative error of at most 0.0069.
The roundings to bfloat16 on the way count: a program that leaves them out, or rounds other values in their place, can miss the bound.
Values may be sent and summed in bfloat16 or wider, within the bound.
No kernel may reach another device: no remote copies, remote signals or barrier semaphores. Data moves between devices by JAX's collectives and lax.ppermute only.
A program may use at most 64 MiB of HBM per device.

v0:
```python
import jax
import jax.numpy as jnp
from jax import lax
from jax.sharding import PartitionSpec as P


def rms_scale(values):
    return lax.rsqrt(jnp.mean(values * values, axis=-1, keepdims=True) + 1e-05)


def pool_masks(ids, counts):
    slots = jnp.arange(counts.shape[0], dtype=jnp.int32)
    member = ids[:, None] == slots[None, :]
    starts = jnp.sum((ids[:, None] < slots[None, :]).astype(jnp.int32), axis=0)
    start_row = jnp.sum(jnp.where(member, starts[None, :], 0), axis=1)
    count_row = jnp.sum(jnp.where(member, counts[None, :], 0), axis=1)
    position = jnp.arange(ids.shape[0], dtype=jnp.int32) - start_row
    valid = (position < count_row).astype(jnp.float32)
    return (member.astype(jnp.float32), valid)


def sum_groups(local_mass):
    return 1.0 + lax.psum(local_mass, "dp")


def body(
    residual,
    ffn_gain,
    gate_weight,
    up_weight,
    down_weight,
    final_gain,
    head_weight,
    passage_ids,
    valid_counts,
):
    highest = lax.Precision.HIGHEST
    own_rows = residual.astype(jnp.float32)
    tok_rows = own_rows.shape[0]
    group_rows = tok_rows * lax.axis_size("mp")
    normed_in = (own_rows * rms_scale(own_rows) * ffn_gain).astype(jnp.bfloat16)
    gathered = lax.all_gather(normed_in, "mp", axis=0, tiled=True)
    offset = lax.axis_index("mp") * tok_rows
    placed = lax.dynamic_update_slice_in_dim(
        jnp.zeros((group_rows, own_rows.shape[1]), jnp.float32), own_rows, offset, 0
    )
    row_block = gathered
    gate_vals = jnp.dot(row_block, gate_weight, preferred_element_type=jnp.float32)
    up_vals = jnp.dot(row_block, up_weight, preferred_element_type=jnp.float32)
    activated = (jax.nn.silu(gate_vals) * up_vals).astype(jnp.bfloat16)
    hidden_all = lax.psum(
        jnp.dot(activated, down_weight, preferred_element_type=jnp.float32) + placed, "mp"
    )
    scale_all = rms_scale(hidden_all)
    normed_all = (hidden_all * scale_all * final_gain).astype(jnp.bfloat16)
    logits = jnp.dot(normed_all, head_weight, preferred_element_type=jnp.float32)
    hidden = lax.dynamic_slice_in_dim(hidden_all, offset, tok_rows, 0)
    scale = lax.dynamic_slice_in_dim(scale_all, offset, tok_rows, 0)
    member, valid = pool_masks(passage_ids[0], valid_counts[0])
    weights = jnp.log1p(jnp.maximum(logits, 0.0))
    powered = valid[:, None] * weights**4
    pooled_sum = lax.dot_general(member, powered, (((0,), (0,)), ((), ())), precision=highest)
    term_weights = (1.0 + pooled_sum) ** 0.25 - 1.0
    local_mass = jnp.sum(term_weights, axis=0)
    smooth = sum_groups(local_mass)
    total = lax.psum(jnp.sum(smooth), "mp")
    spread = lax.psum(jnp.sum(smooth * jnp.log(smooth)), "mp")
    entropy = jnp.log(total) - spread / total
    slope_mass = jnp.log(total) - jnp.log(smooth)
    factor = (1.0 + pooled_sum) ** (-0.75)
    row_factor = jnp.dot(member, factor, precision=highest)
    slope_logit = (
        valid[:, None]
        * weights**3
        * row_factor
        * slope_mass[None, :]
        / (1.0 + jnp.maximum(logits, 0.0))
    ).astype(jnp.bfloat16)
    row_block = slope_logit
    slope_normed = lax.psum_scatter(
        lax.dot_general(
            row_block, head_weight, (((1,), (1,)), ((), ())), preferred_element_type=jnp.float32
        ),
        "mp",
        scatter_dimension=0,
        tiled=True,
    )
    scaled_slope = slope_normed * final_gain
    grad_hidden = scale * scaled_slope - hidden * scale**3 * jnp.mean(
        scaled_slope * hidden, axis=-1, keepdims=True
    )
    return (term_weights, entropy, grad_hidden)


def solution(mesh):
    placed = (
        P(("dp", "mp"), None),
        P(),
        P(None, "mp"),
        P(None, "mp"),
        P("mp", None),
        P(),
        P(None, "mp"),
        P("dp", None),
        P("dp", None),
    )
    return jax.shard_map(
        body,
        mesh=mesh,
        in_specs=placed,
        out_specs=(P("dp", "mp"), P(), P(("dp", "mp"), None)),
        check_vma=False,
    )
```

profile of v0, /device:TPU:2, one launch (start us, length us, event | category | flops | bytes accessed | tf_op | source)
XLA Modules:
  0.0 654.6 jit_solution(14113057163606590066)
XLA Ops:
  7.2 0.0 copy-start
  7.2 0.0 all-gather.3.cloned.1.call-start
  7.2 1.0 fusion.19
  8.2 1.5 fusion.24
  9.7 0.0 all-gather.3.cloned.1.call-update
  9.7 0.0 all-reduce.5.cloned.1.call-start
  9.8 82.1 %all-gather.3.cloned.1.call-done = bf16[64,4,4096]{2,1,0:T(4,128)(2,1)} async-done(((bf16[1,4,4096]{2,1,0:T(4,128)(2,1)}), bf16[64,4,4096]{2,1,0:T(4,128)(2,1)}) %all-gather.3.cloned.1.call-update) | async-done | bytes 2097168 | tf_op jit(solution)/shard_map/all_gather | solution.py:42
  91.9 2.5 reshape.57
  94.5 1.9 fusion.34
  96.4 0.0 copy-done
  96.4 0.0 copy-start.2
  96.4 4.5 fusion.8
  100.9 0.0 copy-done.2
  100.9 0.0 copy-start.4
  100.9 0.0 copy-start.5
  100.9 1.6 fusion.22
  102.5 0.0 copy-start.3
  102.5 0.0 all-reduce.5.cloned.1.call-update
  102.5 0.0 all-reduce.7.cloned.1.call-start
  102.6 0.0 copy-done.4
  102.6 0.1 convert_reduce_fusion
  102.7 0.0 copy-done.5
  102.7 0.1 select_reduce_fusion.1
  102.8 193.2 %all-reduce.5.cloned.1.call-done = f32[256,4096]{1,0:T(8,128)} async-done(((f32[256,4096]{1,0:T(8,128)}), f32[256,4096]{1,0:T(8,128)}) %all-reduce.5.cloned.1.call-update) | async-done | bytes 4194320 | tf_op jit(solution)/shard_map/psum | solution.py:51
  296.1 0.0 copy-start.1
  296.1 2.7 multiply_reduce_fusion
  298.8 0.0 copy-done.3
  298.8 0.7 copy-done.1
  299.5 5.8 fusion.5
  305.3 1.5 fusion.33
  306.8 8.6 %psum.29 = f32[1024]{0:T(1024)S(1)} all-reduce(f32[1024]{0:T(1024)S(1)} %get-tuple-element.11), channel_id=1, replica_groups=mesh['dp'=4,'mp'=64] {'dp'}, use_global_device_ids=true, to_apply=%region_7.8 | all-reduce | flops 1024 | bytes 8192 | tf_op jit(solution)/shard_map/psum | solution.py:23
  315.3 0.6 fusion.27
  315.9 126.2 %all-reduce.1 = (f32[]{:T(128)}, f32[]{:T(128)}) all-reduce(f32[]{:T(128)} %get-tuple-element.4, f32[]{:T(128)} %get-tuple-element.3), channel_id=1, replica_groups=mesh['dp'=4,'mp'=64] {'mp'}, use_global_device_ids=true, to_apply=%region_9.10 | all-reduce | flops 2 | bytes 16 | tf_op jit(solution)/shard_map/psum | solution.py:66
  442.8 1.1 fusion.6
  443.9 7.7 %fusion.35 = f32[256,4096]{1,0:T(8,128)} fusion(bf16[256,1024]{1,0:T(8,128)(2,1)S(1)} %fusion.6, bf16[4096,1024]{1,0:T(8,128)(2,1)} %param.15), kind=kOutput, calls=%fused_computation.61 | convolution fusion | flops 2147483648 | bytes 13107200 | tf_op jit(solution)/shard_map/dot_general | solution.py:81
  451.7 0.0 copy-start.6
  451.7 0.0 all-reduce.7.cloned.1.call-update
  451.7 0.6 copy-done.6
  452.4 0.6 dynamic-slice.5
  454.9 0.1 fusion.30
  455.0 189.1 %all-reduce.7.cloned.1.call-done = f32[256,4096]{1,0:T(8,128)} async-done(((f32[256,4096]{1,0:T(8,128)}), f32[256,4096]{1,0:T(8,128)}) %all-reduce.7.cloned.1.call-update) | async-done | bytes 4194320
  644.1 1.1 multiply_reduce_fusion.1
  645.2 1.7 multiply_subtract_fusion
  (5 shorter events, 0.0 us)
Async XLA Ops:
  7.2 89.2 %copy-start = (bf16[128,4096]{1,0:T(8,128)(2,1)S(1)}, bf16[128,4096]{1,0:T(8,128)(2,1)}, u32[]{:S(2)}) copy-start(bf16[128,4096]{1,0:T(8,128)(2,1)} %param.13) | copy-start | bytes 3145732
  7.2 84.7 %all-gather.3.cloned.1.call-start = ((), (), s32[]{:S(2)}) async-start(), calls=%async_computation.1 | async-start | bytes 2129920 | tf_op jit(solution)/shard_map/all_gather | solution.py:42
  9.7 286.3 %all-reduce.5.cloned.1.call-start = ((), (), s32[]{:S(2)}) async-start(), calls=%async_computation | async-start | bytes 8388608 | tf_op jit(solution)/shard_map/psum | solution.py:51
  96.4 4.5 copy-start.2
  100.9 1.7 copy-start.4
  100.9 1.8 copy-start.5
  102.5 196.2 %copy-start.3 = (f32[4096]{0:T(1024)S(1)}, f32[4096]{0:T(1024)}, u32[]{:S(2)}) copy-start(f32[4096]{0:T(1024)} %param.14) | copy-start | bytes 49156
  102.5 541.5 %all-reduce.7.cloned.1.call-start = ((), (), s32[]{:S(2)}) async-start(), calls=%async_computation.2 | async-start | bytes 8388608
  296.1 3.4 copy-start.1
  451.7 0.7 copy-start.6
Sparse Core Ops, SparseCore 0:
  11.3 80.5 all-gather.2
  102.7 193.3 all-reduce.4
  451.8 192.2 all-reduce.6
where the time goes:
time: 655 us
  waiting for transfers between devices  465 us (71%)
  blocking collectives  135 us (21%)
  matrix products  22.5 us (3%)
  between operations  17.6 us (3%)
  other arithmetic  10.5 us (2%)
    psum x1, waiting for transfers between devices, body(): lax.psum(jnp.dot(activated, down_weight, preferred_element_type=jnp.float...  193 us
    unnamed x4, waiting for transfers between devices  189 us
    psum x1, blocking collectives, body(): total = lax.psum(jnp.sum(smooth), 'mp')  126 us
    all_gather x1, waiting for transfers between devices, body(): gathered = lax.all_gather(normed_in, 'mp', axis=0, tiled=True)  82.1 us
  transfers between devices with their start and end apart: 3, of which 3 were waited for; matrix products, arithmetic and copies ran while one was open for 0% of the time, Pallas kernels for 0%

commit v1 on v0

--- a/solution.py
+++ b/solution.py
@@ -1,7 +1,18 @@
+import functools
 import jax
 import jax.numpy as jnp
 from jax import lax
 from jax.sharding import PartitionSpec as P
+
+
+def handle_the_pairs_all(load, device_axis):
+    return jnp.concatenate(
+        lax.all_to_all(jnp.stack(lax.axis_size(device_axis) * [load], axis=0), device_axis, 0, 0),
+        axis=0,
+    )
+
+
+step_on_sizes = functools.partial(handle_the_pairs_all, device_axis="mp")
 
 
 def rms_scale(values):
@@ -39,7 +50,7 @@
     tok_rows = own_rows.shape[0]
     group_rows = tok_rows * lax.axis_size("mp")
     normed_in = (own_rows * rms_scale(own_rows) * ffn_gain).astype(jnp.bfloat16)
-    gathered = lax.all_gather(normed_in, "mp", axis=0, tiled=True)
+    gathered = step_on_sizes(normed_in)
     offset = lax.axis_index("mp") * tok_rows
     placed = lax.dynamic_update_slice_in_dim(
         jnp.zeros((group_rows, own_rows.shape[1]), jnp.float32), own_rows, offset, 0

time: 655 us -> 637 us (0.973)
  waiting for transfers between devices: 465 us -> 432 us
  starting transfers between devices: 0.12 us -> 12.5 us
    all_gather x1 -> x0, waiting for transfers between devices: 82.1 us -> none  [body(): gathered = lax.all_gather(normed_in, 'mp', axis=0, tiled=True)]
    all_to_all x0 -> x1, waiting for transfers between devices: none -> 51.1 us  [handle_the_pairs_all(): lax.all_to_all(jnp.stack(lax.axis_size(device_axis) * [load], axis=0), de...]
    all_to_all x0 -> x1, starting transfers between devices: none -> 12.4 us  [handle_the_pairs_all(): lax.all_to_all(jnp.stack(lax.axis_size(device_axis) * [load], axis=0), de...]
    unnamed x4 -> x3, waiting for transfers between devices: 189 us -> 189 us
where the time goes in v1:
time: 637 us
  waiting for transfers between devices  432 us (68%)
  blocking collectives  135 us (21%)
  matrix products  22.5 us (4%)
  between operations  17.9 us (3%)
  starting transfers between devices  12.5 us (2%)
  other arithmetic  9.87 us (2%)
  local copies, waits for them, and re-layouts  6.86 us (1%)
    psum x1, waiting for transfers between devices, body(): lax.psum(jnp.dot(activated, down_weight, preferred_element_type=jnp.float...  192 us
    unnamed x3, waiting for transfers between devices  189 us
    psum x1, blocking collectives, body(): total = lax.psum(jnp.sum(smooth), 'mp')  126 us
    all_to_all x1, waiting for transfers between devices, handle_the_pairs_all(): lax.all_to_all(jnp.stack(lax.axis_size(device_axis) * [load], axis=0), de...  51.1 us
  transfers between devices with their start and end apart: 3, of which 3 were waited for; matrix products, arithmetic and copies ran while one was open for 0% of the time, Pallas kernels for 0%

profile of v1, /device:TPU:2, one launch (start us, length us, event | category | flops | bytes accessed | tf_op | source)
XLA Modules:
  0.0 636.9 jit_solution(12310213831496150170)
XLA Ops:
  7.2 0.0 copy-start
  7.2 1.0 fusion.19
  8.2 0.9 fusion.21
  9.0 2.3 stack.2
  11.3 12.4 %all-to-all-start = ((bf16[64,4,4096]{2,1,0:T(4,128)(2,1)}), bf16[64,4,4096]{2,1,0:T(4,128)(2,1)}, u32[]{:S(2)}, u32[]{:S(2)}) async-start(bf16[64,4,4096]{2,1,0:T(4,128)(2,1)} %stack.2), calls=%async_computation | async-start | bytes 4194304 | tf_op jit(solution)/shard_map/all_to_all | solution.py:10
  23.7 0.0 all-reduce.5.cloned.1.call-start
  23.8 51.1 %all-to-all-done = bf16[64,4,4096]{2,1,0:T(4,128)(2,1)} async-done(((bf16[64,4,4096]{2,1,0:T(4,128)(2,1)}), bf16[64,4,4096]{2,1,0:T(4,128)(2,1)}, u32[]{:S(2)}, u32[]{:S(2)}) %all-to-all-start) | async-done | bytes 2097184 | tf_op jit(solution)/shard_map/all_to_all | solution.py:10
  74.9 2.5 reshape.61
  77.4 1.9 fusion.33
  79.4 0.0 copy-done
  79.4 0.0 copy-start.2
  79.4 4.5 fusion.8
  83.9 0.0 copy-done.2
  83.9 0.0 copy-start.4
  83.9 0.0 copy-start.5
  83.9 1.6 fusion.22
  85.5 0.0 copy-start.3
  85.5 0.0 all-reduce.5.cloned.1.call-update
  85.5 0.0 all-reduce.7.cloned.1.call-start
  85.6 0.0 copy-done.4
  85.6 0.1 convert_reduce_fusion
  85.7 0.0 copy-done.5
  85.7 0.1 select_reduce_fusion.1
  85.8 192.3 %all-reduce.5.cloned.1.call-done = f32[256,4096]{1,0:T(8,128)} async-done(((f32[256,4096]{1,0:T(8,128)}), f32[256,4096]{1,0:T(8,128)}) %all-reduce.5.cloned.1.call-update) | async-done | bytes 4194320 | tf_op jit(solution)/shard_map/psum | solution.py:62
  278.1 0.0 copy-start.1
  278.1 2.7 multiply_reduce_fusion
  280.8 0.0 copy-done.3
  280.8 0.7 copy-done.1
  281.5 5.8 fusion.5
  287.3 1.5 fusion.32
  288.8 8.6 %psum.29 = f32[1024]{0:T(1024)S(1)} all-reduce(f32[1024]{0:T(1024)S(1)} %get-tuple-element.11), channel_id=1, replica_groups=mesh['dp'=4,'mp'=64] {'dp'}, use_global_device_ids=true, to_apply=%region_7.8 | all-reduce | flops 1024 | bytes 8192 | tf_op jit(solution)/shard_map/psum | solution.py:34
  297.3 0.6 fusion.26
  297.9 126.2 %all-reduce.1 = (f32[]{:T(128)}, f32[]{:T(128)}) all-reduce(f32[]{:T(128)} %get-tuple-element.4, f32[]{:T(128)} %get-tuple-element.3), channel_id=1, replica_groups=mesh['dp'=4,'mp'=64] {'mp'}, use_global_device_ids=true, to_apply=%region_9.10 | all-reduce | flops 2 | bytes 16 | tf_op jit(solution)/shard_map/psum | solution.py:77
  424.8 1.1 fusion.6
  426.0 7.7 %fusion.34 = f32[256,4096]{1,0:T(8,128)} fusion(bf16[256,1024]{1,0:T(8,128)(2,1)S(1)} %fusion.6, bf16[4096,1024]{1,0:T(8,128)(2,1)} %param.15), kind=kOutput, calls=%fused_computation.60 | convolution fusion | flops 2147483648 | bytes 13107200 | tf_op jit(solution)/shard_map/dot_general | solution.py:92
  433.7 0.0 copy-start.6
  433.7 0.0 all-reduce.7.cloned.1.call-update
  433.7 0.6 copy-done.6
  434.4 0.6 dynamic-slice.5
  436.9 0.1 fusion.29
  437.0 189.1 %all-reduce.7.cloned.1.call-done = f32[256,4096]{1,0:T(8,128)} async-done(((f32[256,4096]{1,0:T(8,128)}), f32[256,4096]{1,0:T(8,128)}) %all-reduce.7.cloned.1.call-update) | async-done | bytes 4194320
  626.1 1.1 multiply_reduce_fusion.1
  627.2 1.7 multiply_subtract_fusion
  (5 shorter events, 0.0 us)
Async XLA Ops:
  7.2 72.2 %copy-start = (bf16[128,4096]{1,0:T(8,128)(2,1)S(1)}, bf16[128,4096]{1,0:T(8,128)(2,1)}, u32[]{:S(2)}) copy-start(bf16[128,4096]{1,0:T(8,128)(2,1)} %param.13) | copy-start | bytes 3145732
  11.3 63.6 %all-to-all-start = ((bf16[64,4,4096]{2,1,0:T(4,128)(2,1)}), bf16[64,4,4096]{2,1,0:T(4,128)(2,1)}, u32[]{:S(2)}, u32[]{:S(2)}) async-start(bf16[64,4,4096]{2,1,0:T(4,128)(2,1)} %stack.2), calls=%async_computation | async-start | bytes 4194304 | tf_op jit(solution)/shard_map/all_to_all | solution.py:10
  23.7 254.4 %all-reduce.5.cloned.1.call-start = ((), (), s32[]{:S(2)}) async-start(), calls=%async_computation.1 | async-start | bytes 8388608 | tf_op jit(solution)/shard_map/psum | solution.py:62
  79.4 4.5 copy-start.2
  83.9 1.7 copy-start.4
  83.9 1.8 copy-start.5
  85.5 195.3 %copy-start.3 = (f32[4096]{0:T(1024)S(1)}, f32[4096]{0:T(1024)}, u32[]{:S(2)}) copy-start(f32[4096]{0:T(1024)} %param.14) | copy-start | bytes 49156
  85.5 540.6 %all-reduce.7.cloned.1.call-start = ((), (), s32[]{:S(2)}) async-start(), calls=%async_computation.2 | async-start | bytes 8388608
  278.1 3.4 copy-start.1
  433.7 0.7 copy-start.6
Sparse Core Ops, SparseCore 0:
  85.7 192.3 all-reduce.4
  433.8 192.2 all-reduce.6
